TPU v7x, 32 devices: a whole 2x2x4 slice. The times are simulated.
32 devices in a mesh: win: 2 (over y), vel: 8 (over z, x), sp: 2 (over core).
Axes of the slice: x: 2, y: 2, z: 4, core: 2. Of those that a mesh axis runs over, the one named last changes fastest.
Arguments:
- f_start: float32 [2, 1536, 64, 128], P('win', 'vel', 'sp'), may hold values from 0 to 15, as said below
- relax_rate: float32 [64, 128], P('sp'), may hold values from 0.1 to 10
Outputs:
- corrected: float32 [2, 4, 64, 128], P('win', None, 'sp')
- lifted: float32 [2, 1536, 64, 128], P('win', 'vel', 'sp')
Inputs may be any that keep to these rules, and one draw needn't show every extreme that they name: `f_start`: no entry is negative.
All inputs are finite; a program needn't handle non-finite values.
Results may differ from a plain program's by a relative error of at most 0.00021.
Values sent between devices are 32-bit elements; how exact they have to be, the bound alone decides.
A program may use at most 64 MiB of HBM per device.

v0:
```python
import math
import jax
import jax.numpy as jnp
from jax import lax
from jax.sharding import PartitionSpec as P

NVX = 48
NVY = 32
vel_max = 6.0
fine_ratio = 0.075
coarse_ratio = 0.15
density_floor = 0.3
thermal_lower_bound = 0.3


def with_halo(block, sides, width):
    for axis, dim in sides:
        count = lax.axis_size(axis)
        forward = [(i, i + 1) for i in range(count - 1)]
        forward.append((count - 1, 0))
        backward = [(target, source) for source, target in forward]
        low = lax.ppermute(
            lax.slice_in_dim(block, block.shape[dim] - width, None, axis=dim), axis, forward
        )
        high = lax.ppermute(lax.slice_in_dim(block, 0, width, axis=dim), axis, backward)
        block = jnp.concatenate([low, block, high], axis=dim)
    return block


def shifted(value, axis, steps):
    count = lax.axis_size(axis)
    leading, last = (max(0, -steps), min(count, count - steps))
    return lax.ppermute(value, axis, [(source, source + steps) for source in range(leading, last)])


def velocity_table(first, count):
    index = first + jnp.arange(count, dtype=jnp.int32)
    vel_x = -vel_max + ((index // NVY).astype(jnp.float32) + 0.5) * (2.0 * vel_max / NVX)
    vel_y = -vel_max + ((index % NVY).astype(jnp.float32) + 0.5) * (2.0 * vel_max / NVY)
    return (vel_x, vel_y)


def moment_table(vel_x, vel_y):
    weight_unit = 2.0 * vel_max / NVX * (2.0 * vel_max / NVY) / (2.0 * math.pi)
    return (
        jnp.stack([jnp.ones_like(vel_x), vel_x, vel_y, 0.5 * (vel_x * vel_x + vel_y * vel_y)])
        * weight_unit
    )


def moments(field, table):
    flat = field.reshape(field.shape[0], -1)
    out = jnp.dot(table, flat, precision=lax.Precision.HIGHEST, preferred_element_type=jnp.float32)
    return out.reshape(4, field.shape[1], field.shape[2])


def physical_variables(distribution_array):
    mass_per_volume = jnp.maximum(distribution_array[0], density_floor)
    horizontal_flow = distribution_array[1] / mass_per_volume
    upward_flow = distribution_array[2] / mass_per_volume
    inner_volumes = (
        distribution_array[3]
        - 0.5 * (distribution_array[1] * horizontal_flow + distribution_array[2] * upward_flow)
    ) / mass_per_volume
    pointwise_thermal_level = jnp.maximum(inner_volumes, thermal_lower_bound)
    return (mass_per_volume, horizontal_flow, upward_flow, pointwise_thermal_level)


def equilibrium_density(distribution_array, vel_x, vel_y):
    mass_per_volume, horizontal_flow, upward_flow, pointwise_thermal_level = physical_variables(
        distribution_array
    )
    horizontal_gradient = vel_x[:, None, None] - horizontal_flow[None]
    upward_gradient = vel_y[:, None, None] - upward_flow[None]
    return (mass_per_volume / pointwise_thermal_level)[None] * jnp.exp(
        -(horizontal_gradient * horizontal_gradient + upward_gradient * upward_gradient)
        / (2.0 * pointwise_thermal_level[None])
    )


def transport(field, left, right, vel_x, vel_y):
    coef_x = (vel_x * fine_ratio)[:, None, None]
    coef_y = (vel_y * fine_ratio)[:, None, None]
    below = jnp.roll(field, 1, axis=2)
    above = jnp.roll(field, -1, axis=2)
    out = (
        field
        - jnp.maximum(coef_x, 0.0) * (field - left)
        - jnp.minimum(coef_x, 0.0) * (right - field)
    )
    return (
        out
        - jnp.maximum(coef_y, 0.0) * (field - below)
        - jnp.minimum(coef_y, 0.0) * (above - field)
    )


def euler_update(padded_array):
    mass_per_volume, horizontal_flow, upward_flow, pointwise_thermal_level = physical_variables(
        padded_array
    )
    normal_stress = mass_per_volume * pointwise_thermal_level
    acoustic_wave_rate = jnp.sqrt(2.0 * pointwise_thermal_level)
    flux_x = jnp.stack(
        [
            padded_array[1],
            padded_array[1] * horizontal_flow + normal_stress,
            padded_array[2] * horizontal_flow,
            (padded_array[3] + normal_stress) * horizontal_flow,
        ]
    )
    flux_y = jnp.stack(
        [
            padded_array[2],
            padded_array[1] * upward_flow,
            padded_array[2] * upward_flow + normal_stress,
            (padded_array[3] + normal_stress) * upward_flow,
        ]
    )
    reach_x = jnp.abs(horizontal_flow) + acoustic_wave_rate
    reach_y = jnp.abs(upward_flow) + acoustic_wave_rate
    face_x = 0.5 * (flux_x[:, :-1, 1:-1] + flux_x[:, 1:, 1:-1]) - 0.5 * jnp.maximum(
        reach_x[:-1, 1:-1], reach_x[1:, 1:-1]
    )[None] * (padded_array[:, 1:, 1:-1] - padded_array[:, :-1, 1:-1])
    face_y = 0.5 * (flux_y[:, 1:-1, :-1] + flux_y[:, 1:-1, 1:]) - 0.5 * jnp.maximum(
        reach_y[1:-1, :-1], reach_y[1:-1, 1:]
    )[None] * (padded_array[:, 1:-1, 1:] - padded_array[:, 1:-1, :-1])
    return padded_array[:, 1:-1, 1:-1] - coarse_ratio * (
        face_x[:, 1:] - face_x[:, :-1] + (face_y[:, :, 1:] - face_y[:, :, :-1])
    )


def coarse_step(distribution_array):
    padded_array = with_halo(distribution_array, (("sp", 1),), 1)
    padded_array = jnp.concatenate(
        [padded_array[:, :, -1:], padded_array, padded_array[:, :, :1]], axis=2
    )
    return euler_update(padded_array)


def advance(current, vel_x, vel_y):
    padded_array = with_halo(current, (("sp", 1),), 1)
    return transport(current, padded_array[:, :-2], padded_array[:, 2:], vel_x, vel_y)


def per_device(f_start, relax_rate):
    field = f_start[0]
    count = field.shape[0]
    vel_x, vel_y = velocity_table(lax.axis_index("vel") * count, count)
    table = moment_table(vel_x, vel_y)
    rates = relax_rate[None]
    local_start = moments(field, table)
    start = lax.psum(local_start, "vel")
    current = field
    for step in range(2):
        star = advance(current, vel_x, vel_y)
        distribution_array = lax.psum(moments(star, table), "vel")
        current = (star + rates * equilibrium_density(distribution_array, vel_x, vel_y)) / (
            1.0 + rates
        )
    delta = distribution_array - coarse_step(start)
    windows = lax.axis_size("win")
    position = lax.axis_index("win")
    carried = start
    for turn in range(windows):
        result = coarse_step(carried) + delta
        if turn + 1 < windows:
            passed = shifted(result, "win", 1)
            carried = jnp.where(position == 0, start, passed)
    lifted = (
        current
        + equilibrium_density(result, vel_x, vel_y)
        - equilibrium_density(distribution_array, vel_x, vel_y)
    )
    return (result[None], lifted[None])


def solution(mesh):
    return jax.shard_map(
        per_device,
        mesh=mesh,
        in_specs=(P("win", "vel", "sp", None), P("sp", None)),
        out_specs=(P("win", None, "sp", None), P("win", "vel", "sp", None)),
        check_vma=False,
    )
```

profile of v0, /device:TPU:0, one launch (start us, length us, event | category | flops | bytes accessed | tf_op | source)
XLA Modules:
  0.0 217.6 jit_solution(6024811357756668443)
XLA Ops:
  7.2 2.2 fusion.107
  9.4 0.5 collective-permute-start.2
  9.9 6.6 %fusion.105 = (f32[192,32,127]{2,1,0:T(8,128)}, f32[192,32,127]{2,1,0:T(8,128)}) fusion(f32[192,32,128]{2,1,0:T(8,128)} %bitcast.194), kind=kLoop, calls=%fused_computation.217 | loop fusion | bytes 12484608 | tf_op jit(solution)/shard_map/jit(_roll_static)/slice | solution.py:85
  16.5 3.9 %fusion.106 = (f32[192,32,1]{2,1,0:T(8,128)}, f32[192,32,1]{2,1,0:T(8,128)}) fusion(f32[192,32,128]{2,1,0:T(8,128)S(1)} %bitcast.195), kind=kLoop, calls=%fused_computation.218 | loop fusion | bytes 98304 | tf_op jit(solution)/shard_map/jit(_roll_static)/slice | solution.py:85
  20.4 3.9 %fusion.6 = f32[4,32,128]{2,0,1:T(4,128)} fusion(f32[1,192]{1,0:T(1,128)S(1)} %get-tuple-element.77, f32[1,192]{1,0:T(1,128)S(1)} %get-tuple-element.76, f32[1,192]{1,0:T(1,128)S(1)} %multiply_add_fusion.4, f32[4]{0:T(128)S(1)} %pad.72.clone, f32[24,8,32,128]{3,2,1,0:T(8,128)S(1)} %bitcast.196), kind=kOutput, calls=%fused_computation.9 | convolution fusion | flops 37751808 | bytes 3213584 | tf_op jit(solution)/shard_map/dot_general | solution.py:53
  24.4 6.2 %fusion.21 = f32[192,32,128]{2,1,0:T(8,128)S(1)} fusion(f32[192,32,128]{2,1,0:T(8,128)S(1)} %bitcast.197, f32[192,1,128]{2,1,0:T(1,128)S(1)} %collective-permute-done.3, f32[192,1,128]{2,1,0:T(1,128)S(1)} %collective-permute-done.2, f32[192,32,127]{2,1,0:T(8,128)} %get-tuple-element.42, f32[192,32,1]{2,1,0:T(8,128)} %get-tuple-element.44, ...), kind=kLoop, calls=%fused_computation.27 | loop fusion | flops 12582912 | bytes 12782592 | tf_op jit(solution)/shard_map/sub | solution.py:92
  30.7 1.7 copy-done.1
  32.3 3.9 %fusion.3 = f32[4,32,128]{2,0,1:T(4,128)} fusion(f32[1,192]{1,0:T(1,128)S(1)} %get-tuple-element.77, f32[1,192]{1,0:T(1,128)S(1)} %get-tuple-element.76, f32[1,192]{1,0:T(1,128)S(1)} %multiply_add_fusion.4, f32[4]{0:T(128)S(1)} %pad.72.clone, f32[24,8,32,128]{3,2,1,0:T(8,128)S(1)} %bitcast.199), kind=kOutput, calls=%fused_computation.6 | convolution fusion | flops 37751808 | bytes 3213584 | tf_op jit(solution)/shard_map/dot_general | solution.py:53
  36.3 0.2 all-reduce.6.cloned.1.call-start
  36.5 71.9 %all-reduce.4.cloned.1.call-done = f32[4,32,128]{2,0,1:T(4,128)} async-done(((f32[4,32,128]{2,0,1:T(4,128)}), f32[4,32,128]{2,0,1:T(4,128)}) %all-reduce.4.cloned.1.call-update) | async-done | bytes 65552 | tf_op jit(solution)/shard_map/psum | solution.py:157
  108.4 1.1 fusion.90
  109.5 2.9 %add_divide_fusion = f32[192,32,128]{2,1,0:T(8,128)S(1)} fusion(f32[192,32,128]{2,1,0:T(8,128)} %copy-done.1, f32[32,128]{1,0:T(8,128)S(1)} %broadcast_add_fusion, f32[32,128]{1,0:T(8,128)S(1)} %bitcast.210, f32[32,128]{1,0:T(8,128)S(1)} %bitcast.219, f32[192]{0:T(256)S(1)} %get-tuple-element.78, f32[32,128]{1,0:T(8,128)S(1)} %bitcast.218, ...), kind=kLoop, calls=%fused_computation.41 | loop fusion | flops 8650752 | bytes 6391296 | tf_op jit(solution)/shard_map/div | solution.py:158
  112.4 1.1 fusion.102
  113.5 0.1 fusion.104
  113.7 0.5 collective-permute-start.5
  114.2 1.1 fusion.103
  115.4 3.9 %fusion.13 = f32[192,32,128]{2,1,0:T(8,128)S(1)} fusion(f32[192,32,128]{2,1,0:T(8,128)S(1)} %add_divide_fusion, f32[192,1,128]{2,1,0:T(1,128)S(1)} %collective-permute-done.5, f32[192,1,128]{2,1,0:T(1,128)S(1)} %collective-permute-done.4, f32[192,32,127]{2,1,0:T(8,128)S(1)} %get-tuple-element.36, f32[192,32,1]{2,1,0:T(8,128)S(1)} %get-tuple-element.38, ...), kind=kLoop, calls=%fused_computation.17 | loop fusion | flops 12582912 | bytes 12782592 | tf_op jit(solution)/shard_map/sub | solution.py:92
  119.3 3.9 %fusion = f32[4,32,128]{2,0,1:T(4,128)} fusion(f32[1,192]{1,0:T(1,128)S(1)} %get-tuple-element.77, f32[1,192]{1,0:T(1,128)S(1)} %get-tuple-element.76, f32[1,192]{1,0:T(1,128)S(1)} %multiply_add_fusion.4, f32[4]{0:T(128)S(1)} %pad.72.clone, f32[24,8,32,128]{3,2,1,0:T(8,128)S(1)} %bitcast.198), kind=kOutput, calls=%fused_computation.3 | convolution fusion | flops 37751808 | bytes 3213584 | tf_op jit(solution)/shard_map/dot_general | solution.py:53
  123.2 70.8 %all-reduce.6.cloned.1.call-done = (f32[4,32,128]{2,0,1:T(4,128)}, f32[4,32,128]{2,0,1:T(4,128)}) async-done(((f32[4,32,128]{2,0,1:T(4,128)}, f32[4,32,128]{2,0,1:T(4,128)}), (f32[4,32,128]{2,0,1:T(4,128)}, f32[4,32,128]{2,0,1:T(4,128)})) %all-reduce.6.cloned.1.call-update) | async-done | bytes 131088 | tf_op jit(solution)/shard_map/psum | solution.py:157
  194.0 0.7 fusion.113
  194.8 0.5 collective-permute-start.1
  195.3 0.8 copy.29
  196.2 0.1 fusion.110
  196.2 0.2 pad_maximum_fusion.4
  196.5 0.1 slice_add_fusion.2
  196.8 0.1 slice_add_fusion.1
  197.0 0.1 fusion.34
  197.1 0.2 copy_subtract_fusion
  197.3 0.1 fusion.97
  197.5 3.4 %collective-permute-start.6 = (f32[4,32,128]{2,0,1:T(4,128)S(1)}, f32[4,32,128]{2,0,1:T(4,128)S(1)}, u32[]{:S(2)}, u32[]{:S(2)}) collective-permute-start(f32[4,32,128]{2,0,1:T(4,128)S(1)} %get-tuple-element.23), channel_id=1, source_target_pairs={{0,16},{1,17},{2,18},{3,19},{4,20},{5,21},{6,22},{7,23},{8,24},{9,... | collective-permute-start | bytes 196616 | tf_op jit(solution)/shard_map/ppermute | solution.py:33
  200.8 0.1 fusion.91
  200.9 1.8 collective-permute-done.6
  202.8 0.5 collective-permute-start.8
  203.4 0.6 collective-permute-done.7
  204.0 0.2 collective-permute-done.8
  204.2 0.1 fusion.111
  204.3 0.2 pad_maximum_fusion.7
  204.5 0.1 fusion.109
  204.6 0.2 fusion.93
  204.8 0.1 slice_multiply_fusion.3
  205.1 0.1 fusion.64
  205.3 0.1 pad_maximum_fusion.8
  205.4 0.2 fusion.31
  205.6 0.4 fusion.37
  206.0 0.1 fusion.44
  206.1 0.1 fusion.92
  206.2 0.6 copy.52
  206.9 3.8 %subtract_bitcast_fusion = f32[1,192,32,128]{3,2,1,0:T(8,128)} fusion(f32[192,32,128]{2,1,0:T(8,128)S(1)} %fusion.13, f32[32,128]{1,0:T(8,128)S(1)} %bitcast.209, f32[32,128]{1,0:T(8,128)S(1)} %bitcast.216, f32[32,128]{1,0:T(8,128)S(1)} %bitcast.215, f32[32,128]{1,0:T(8,128)S(1)} %bitcast.214, f32[32,128]{1,0:T(8,128)S(1)} %bitcast.208, ...), kind=kLoop, calls=%fused_computation.40 | loop fusion | flops 16515072 | bytes 6456832 | tf_op jit(solution)/shard_map/broadcast_in_dim | solution.py:175
  (54 shorter events, 1.1 us)
Async XLA Ops:
  7.2 101.2 %all-reduce.4.cloned.1.call-start = ((), (), s32[]{:S(2)}) async-start(), calls=%async_computation | async-start | bytes 131072 | tf_op jit(solution)/shard_map/psum | solution.py:157
  9.4 15.0 %collective-permute-start.2 = (f32[192,1,128]{2,1,0:T(1,128)}, f32[192,1,128]{2,1,0:T(1,128)S(1)}, u32[]{:S(2)}, u32[]{:S(2)}) collective-permute-start(f32[192,1,128]{2,1,0:T(1,128)} %get-tuple-element.45), channel_id=1, source_target_pairs={{0,1},{1,0},{2,3},{3,2},{4,5},{5,4},{6,7},{7,6},{8,9},{9,8},{10,11... | collective-permute-start | bytes 294920 | tf_op jit(solution)/shard_map/ppermute | solution.py:22
  9.9 14.5 %collective-permute-start.3 = (f32[192,1,128]{2,1,0:T(1,128)S(1)}, f32[192,1,128]{2,1,0:T(1,128)S(1)}, u32[]{:S(2)}, u32[]{:S(2)}) collective-permute-start(f32[192,1,128]{2,1,0:T(1,128)S(1)} %get-tuple-element.46), channel_id=1, source_target_pairs={{1,0},{0,1},{3,2},{2,3},{5,4},{4,5},{7,6},{6,7},{9,8},{8,9},{11,10... | collective-permute-start | bytes 294920 | tf_op jit(solution)/shard_map/ppermute | solution.py:25
  9.9 6.6 %copy-start = (f32[1,192,32,128]{3,2,1,0:T(8,128)S(1)}, f32[1,192,32,128]{3,2,1,0:T(8,128)}, u32[]{:S(2)}) copy-start(f32[1,192,32,128]{3,2,1,0:T(8,128)} %param.2) | copy-start | bytes 9437188
  16.5 3.9 %copy-start.5 = (f32[32,128]{1,0:T(8,128)S(1)}, f32[32,128]{1,0:T(8,128)}, u32[]{:S(2)}) copy-start(f32[32,128]{1,0:T(8,128)} %param.3) | copy-start | bytes 49156
  20.3 4.1 %copy-start.2 = (f32[192,32,127]{2,1,0:T(8,128)S(1)}, f32[192,32,127]{2,1,0:T(8,128)}, u32[]{:S(2)}) copy-start(f32[192,32,127]{2,1,0:T(8,128)} %get-tuple-element.41) | copy-start | bytes 9363460
  30.6 1.7 copy-start.1
  36.3 157.8 %all-reduce.6.cloned.1.call-start = ((), (), s32[]{:S(2)}) async-start(), calls=%async_computation.1 | async-start | bytes 262144 | tf_op jit(solution)/shard_map/psum | solution.py:157
  113.7 1.7 collective-permute-start.4
  113.7 1.6 collective-permute-start.5
  194.0 3.3 %copy-start.3 = (f32[4,32,128]{2,0,1:T(4,128)S(1)}, f32[4,32,128]{2,0,1:T(4,128)}, u32[]{:S(2)}) copy-start(f32[4,32,128]{2,0,1:T(4,128)} %get-tuple-element.7) | copy-start | bytes 196612
  194.0 3.3 %copy-start.4 = (f32[4,32,128]{2,0,1:T(4,128)S(1)}, f32[4,32,128]{2,0,1:T(4,128)}, u32[]{:S(2)}) copy-start(f32[4,32,128]{2,0,1:T(4,128)} %get-tuple-element.6) | copy-start | bytes 196612
  194.8 1.4 collective-permute-start
  194.8 1.4 collective-permute-start.1
  197.5 5.3 %collective-permute-start.6 = (f32[4,32,128]{2,0,1:T(4,128)S(1)}, f32[4,32,128]{2,0,1:T(4,128)S(1)}, u32[]{:S(2)}, u32[]{:S(2)}) collective-permute-start(f32[4,32,128]{2,0,1:T(4,128)S(1)} %get-tuple-element.23), channel_id=1, source_target_pairs={{0,16},{1,17},{2,18},{3,19},{4,20},{5,21},{6,22},{7,23},{8,24},{9,... | collective-permute-start | bytes 196616 | tf_op jit(solution)/shard_map/ppermute | solution.py:33
  202.8 1.2 collective-permute-start.7
  202.8 1.3 collective-permute-start.8
Sparse Core Ops, SparseCore 0:
  36.4 71.9 all-reduce.3
  123.3 70.6 all-reduce.5
where the time goes:
time: 218 us
  waiting for transfers between devices  145 us (67%)
  other arithmetic  21.1 us (10%)
  local copies, waits for them, and re-layouts  19.1 us (9%)
  between operations  14.5 us (7%)
  matrix products  11.8 us (5%)
  starting transfers between devices  5.8 us (3%)
    psum x2, waiting for transfers between devices, per_device(): distribution_array = lax.psum(moments(star, table), 'vel')  143 us
    slice x4, local copies, waits for them, and re-layouts, transport(): above = jnp.roll(field, -1, axis=2)  12.6 us
    dot_general x3, matrix products, moments(): jnp.dot(table, flat, precision=lax.Precision.HIGHEST, preferred_element_t...  11.8 us
    sub x2, other arithmetic, transport(): out - jnp.maximum(coef_y, 0.0) * (field - below)  10.1 us
  transfers between devices with their start and end apart: 11, of which 5 were waited for; matrix products, arithmetic and copies ran while one was open for 8% of the time, Pallas kernels for 0%

commit v1 on v0

--- a/solution.py
+++ b/solution.py
@@ -154,7 +154,7 @@
     current = field
     for step in range(2):
         star = advance(current, vel_x, vel_y)
-        distribution_array = lax.psum(moments(star, table), "vel")
+        distribution_array = jnp.sum(lax.all_gather(moments(star, table), "vel"), axis=0)
         current = (star + rates * equilibrium_density(distribution_array, vel_x, vel_y)) / (
             1.0 + rates
         )

time: 218 us -> 204 us (0.936)
  waiting for transfers between devices: 145 us -> 67.5 us
  blocking collectives: 0 us -> 65 us
  local copies, waits for them, and re-layouts: 19.1 us -> 16.5 us
    psum x2 -> x1, waiting for transfers between devices: 143 us -> 64.5 us  [per_device(): start = lax.psum(local_start, 'vel')]
    all_gather x0 -> x2, blocking collectives: none -> 65 us  [per_device(): lax.all_gather(moments(star, table), 'vel')]
    slice x4, local copies, waits for them, and re-layouts: 12.6 us -> 9.78 us  [transport(): above = jnp.roll(field, -1, axis=2)]
  transfers between devices with their start and end apart: 11 -> 10, of which waited for: 5 -> 4; matrix products, arithmetic and copies ran while one was open for 8% -> 8% of each run, Pallas kernels for 0% -> 0%
where the time goes in v1:
time: 204 us
  waiting for transfers between devices  67.5 us (33%)
  blocking collectives  65 us (32%)
  other arithmetic  22.6 us (11%)
  local copies, waits for them, and re-layouts  16.5 us (8%)
  between operations  14.5 us (7%)
  matrix products  12.3 us (6%)
  starting transfers between devices  5.57 us (3%)
    all_gather x2, blocking collectives, per_device(): lax.all_gather(moments(star, table), 'vel')  65 us
    psum x1, waiting for transfers between devices, per_device(): start = lax.psum(local_start, 'vel')  64.5 us
    dot_general x3, matrix products, moments(): jnp.dot(table, flat, precision=lax.Precision.HIGHEST, preferred_element_t...  12.3 us
    sub x2, other arithmetic, transport(): out - jnp.maximum(coef_y, 0.0) * (field - below)  10.2 us
    slice x4, local copies, waits for them, and re-layouts, transport(): above = jnp.roll(field, -1, axis=2)  9.78 us
    broadcast_in_dim x1, other arithmetic, per_device(): return (result[None], lifted[None])  4.56 us
  transfers between devices with their start and end apart: 10, of which 4 were waited for; matrix products, arithmetic and copies ran while one was open for 8% of the time, Pallas kernels for 0%

profile of v1, /device:TPU:0, one launch (start us, length us, event | category | flops | bytes accessed | tf_op | source)
XLA Modules:
  0.0 204.1 jit_solution(4428475189332983849)
XLA Ops:
  7.2 2.3 %fusion.110 = (f32[192,1,128]{2,1,0:T(1,128)}, f32[192,1,128]{2,1,0:T(1,128)}) fusion(f32[192,32,128]{2,1,0:T(8,128)} %bitcast.201), kind=kLoop, calls=%fused_computation.218 | loop fusion | bytes 393216 | tf_op jit(solution)/shard_map/slice | solution.py:23
  9.6 0.5 collective-permute-start.2
  10.1 5.7 %fusion.6 = f32[4,32,128]{2,0,1:T(4,128)} fusion(f32[1,192]{1,0:T(1,128)S(1)} %get-tuple-element.87, f32[1,192]{1,0:T(1,128)S(1)} %get-tuple-element.86, f32[1,192]{1,0:T(1,128)S(1)} %multiply_add_fusion.4, f32[4]{0:T(128)S(1)} %pad.72.clone, f32[24,8,32,128]{3,2,1,0:T(8,128)} %bitcast.202), kind=kOutput, calls=%fused_computation.9 | convolution fusion | flops 37751808 | bytes 3213584 | tf_op jit(solution)/shard_map/dot_general | solution.py:53
  15.9 3.8 %fusion.108 = (f32[192,32,127]{2,1,0:T(8,128)}, f32[192,32,127]{2,1,0:T(8,128)}) fusion(f32[192,32,128]{2,1,0:T(8,128)S(1)} %bitcast.203), kind=kLoop, calls=%fused_computation.216 | loop fusion | bytes 12484608 | tf_op jit(solution)/shard_map/jit(_roll_static)/slice | solution.py:85
  19.7 3.8 %fusion.109 = (f32[192,32,1]{2,1,0:T(8,128)}, f32[192,32,1]{2,1,0:T(8,128)}) fusion(f32[192,32,128]{2,1,0:T(8,128)S(1)} %bitcast.204), kind=kLoop, calls=%fused_computation.217 | loop fusion | bytes 98304 | tf_op jit(solution)/shard_map/jit(_roll_static)/slice | solution.py:85
  23.5 64.5 %all-reduce.2.cloned.1.call-done = f32[4,32,128]{2,0,1:T(4,128)} async-done(((f32[4,32,128]{2,0,1:T(4,128)}), f32[4,32,128]{2,0,1:T(4,128)}) %all-reduce.2.cloned.1.call-update) | async-done | bytes 65552 | tf_op jit(solution)/shard_map/psum | solution.py:153
  88.0 0.8 fusion.118
  88.8 0.5 collective-permute-start.1
  89.4 0.8 copy.83
  90.2 0.1 fusion.113
  90.3 0.2 pad_maximum_fusion.4
  90.6 0.1 slice_add_fusion.1
  90.8 0.1 fusion.34
  91.0 0.1 slice_add_fusion.2
  91.2 0.2 copy_subtract_fusion
  91.4 6.3 %fusion.21 = f32[192,32,128]{2,1,0:T(8,128)S(1)} fusion(f32[192,32,128]{2,1,0:T(8,128)S(1)} %bitcast.205, f32[192,1,128]{2,1,0:T(1,128)} %collective-permute-done.3, f32[192,1,128]{2,1,0:T(1,128)} %collective-permute-done.2, f32[192,32,127]{2,1,0:T(8,128)} %get-tuple-element.44, f32[192,32,1]{2,1,0:T(8,128)} %get-tuple-element.46, ...), kind=kLoop, calls=%fused_computation.27 | loop fusion | flops 12582912 | bytes 12782592 | tf_op jit(solution)/shard_map/sub | solution.py:92
  97.7 1.7 copy-done.1
  99.4 3.3 %fusion.3 = f32[4,32,128]{2,0,1:T(4,128)S(1)} fusion(f32[1,192]{1,0:T(1,128)S(1)} %get-tuple-element.87, f32[1,192]{1,0:T(1,128)S(1)} %get-tuple-element.86, f32[1,192]{1,0:T(1,128)S(1)} %multiply_add_fusion.4, f32[4]{0:T(128)S(1)} %pad.72.clone, f32[24,8,32,128]{3,2,1,0:T(8,128)S(1)} %bitcast.207), kind=kOutput, calls=%fused_computation.6 | convolution fusion | flops 37751808 | bytes 3213584 | tf_op jit(solution)/shard_map/dot_general | solution.py:53
  102.7 31.7 %all-gather = f32[32,32,128]{2,1,0:T(8,128)S(1)} all-gather(f32[4,32,128]{2,1,0:T(8,128)S(1)} %copy.91), channel_id=2, replica_groups=mesh['win'=2,'vel'=8,'sp'=2] {'vel'}, dimensions={0}, use_global_device_ids=true | all-gather | bytes 589824 | tf_op jit(solution)/shard_map/all_gather | solution.py:157
  134.6 2.9 %add_divide_fusion = f32[192,32,128]{2,1,0:T(8,128)S(1)} fusion(f32[192,32,128]{2,1,0:T(8,128)} %copy-done.1, f32[32,128]{1,0:T(8,128)S(1)} %broadcast_add_fusion, f32[32,128]{1,0:T(8,128)S(1)} %bitcast.220, f32[32,128]{1,0:T(8,128)S(1)} %bitcast.229, f32[192]{0:T(256)S(1)} %get-tuple-element.88, f32[32,128]{1,0:T(8,128)S(1)} %bitcast.228, ...), kind=kLoop, calls=%fused_computation.41 | loop fusion | flops 8650752 | bytes 6391296 | tf_op jit(solution)/shard_map/div | solution.py:158
  137.5 1.1 fusion.105
  138.6 0.1 fusion.107
  138.9 0.5 collective-permute-start.5
  139.4 1.1 fusion.106
  140.5 3.9 %fusion.13 = f32[192,32,128]{2,1,0:T(8,128)S(1)} fusion(f32[192,32,128]{2,1,0:T(8,128)S(1)} %add_divide_fusion, f32[192,1,128]{2,1,0:T(1,128)S(1)} %collective-permute-done.5, f32[192,1,128]{2,1,0:T(1,128)S(1)} %collective-permute-done.4, f32[192,32,127]{2,1,0:T(8,128)S(1)} %get-tuple-element.38, f32[192,32,1]{2,1,0:T(8,128)S(1)} %get-tuple-element.40, ...), kind=kLoop, calls=%fused_computation.17 | loop fusion | flops 12582912 | bytes 12782592 | tf_op jit(solution)/shard_map/sub | solution.py:92
  144.4 3.3 %fusion = f32[4,32,128]{2,0,1:T(4,128)S(1)} fusion(f32[1,192]{1,0:T(1,128)S(1)} %get-tuple-element.87, f32[1,192]{1,0:T(1,128)S(1)} %get-tuple-element.86, f32[1,192]{1,0:T(1,128)S(1)} %multiply_add_fusion.4, f32[4]{0:T(128)S(1)} %pad.72.clone, f32[24,8,32,128]{3,2,1,0:T(8,128)S(1)} %bitcast.206), kind=kOutput, calls=%fused_computation.3 | convolution fusion | flops 37751808 | bytes 3213584 | tf_op jit(solution)/shard_map/dot_general | solution.py:53
  147.7 33.3 %all-gather.1 = f32[32,32,128]{2,1,0:T(8,128)} all-gather(f32[4,32,128]{2,1,0:T(8,128)S(1)} %copy.97), channel_id=3, replica_groups=mesh['win'=2,'vel'=8,'sp'=2] {'vel'}, dimensions={0}, use_global_device_ids=true | all-gather | bytes 589824 | tf_op jit(solution)/shard_map/all_gather | solution.py:157
  181.0 1.1 reduce_sum.19
  182.1 0.8 fusion.91
  182.8 3.4 %collective-permute-start.6 = (f32[4,32,128]{2,0,1:T(4,128)}, f32[4,32,128]{2,0,1:T(4,128)S(1)}, u32[]{:S(2)}, u32[]{:S(2)}) collective-permute-start(f32[4,32,128]{2,0,1:T(4,128)} %get-tuple-element.25), channel_id=1, source_target_pairs={{0,16},{1,17},{2,18},{3,19},{4,20},{5,21},{6,22},{7,23},{8,24},{9,... | collective-permute-start | bytes 196616 | tf_op jit(solution)/shard_map/ppermute | solution.py:33
  186.2 2.2 %collective-permute-done.6 = f32[4,32,128]{2,0,1:T(4,128)S(1)} collective-permute-done((f32[4,32,128]{2,0,1:T(4,128)}, f32[4,32,128]{2,0,1:T(4,128)S(1)}, u32[]{:S(2)}, u32[]{:S(2)}) %collective-permute-start.6) | collective-permute-done | bytes 65568 | tf_op jit(solution)/shard_map/ppermute | solution.py:33
  188.5 0.5 collective-permute-start.8
  189.0 0.6 collective-permute-done.7
  189.6 0.2 collective-permute-done.8
  189.8 0.1 fusion.114
  189.9 0.2 pad_maximum_fusion.7
  190.1 0.1 fusion.112
  190.2 0.2 fusion.94
  190.4 0.1 slice_multiply_fusion.3
  190.8 0.1 fusion.64
  190.9 0.1 pad_maximum_fusion.8
  191.1 0.2 fusion.31
  191.3 0.4 fusion.37
  191.7 0.1 fusion.115
  191.8 0.1 fusion.90
  191.9 0.1 fusion.93
  192.0 0.6 copy.117
  192.7 4.6 %subtract_bitcast_fusion = f32[1,192,32,128]{3,2,1,0:T(8,128)} fusion(f32[192,32,128]{2,1,0:T(8,128)S(1)} %fusion.13, f32[32,128]{1,0:T(8,128)S(1)} %bitcast.219, f32[32,128]{1,0:T(8,128)S(1)} %bitcast.226, f32[32,128]{1,0:T(8,128)S(1)} %bitcast.225, f32[32,128]{1,0:T(8,128)S(1)} %bitcast.224, f32[32,128]{1,0:T(8,128)S(1)} %bitcast.218, ...), kind=kLoop, calls=%fused_computation.40 | loop fusion | flops 16515072 | bytes 6456832 | tf_op jit(solution)/shard_map/broadcast_in_dim | solution.py:175
  (59 shorter events, 1.2 us)
Async XLA Ops:
  7.2 8.7 %copy-start = (f32[1,192,32,128]{3,2,1,0:T(8,128)S(1)}, f32[1,192,32,128]{3,2,1,0:T(8,128)}, u32[]{:S(2)}) copy-start(f32[1,192,32,128]{3,2,1,0:T(8,128)} %param.2) | copy-start | bytes 9437188
  7.2 80.8 %all-reduce.2.cloned.1.call-start = ((), (), s32[]{:S(2)}) async-start(), calls=%async_computation | async-start | bytes 131072 | tf_op jit(solution)/shard_map/psum | solution.py:153
  9.6 81.8 %collective-permute-start.2 = (f32[192,1,128]{2,1,0:T(1,128)}, f32[192,1,128]{2,1,0:T(1,128)}, u32[]{:S(2)}, u32[]{:S(2)}) collective-permute-start(f32[192,1,128]{2,1,0:T(1,128)} %get-tuple-element.47), channel_id=1, source_target_pairs={{0,1},{1,0},{2,3},{3,2},{4,5},{5,4},{6,7},{7,6},{8,9},{9,8},{10,11... | collective-permute-start | bytes 294920 | tf_op jit(solution)/shard_map/ppermute | solution.py:22
  10.1 81.4 %collective-permute-start.3 = (f32[192,1,128]{2,1,0:T(1,128)}, f32[192,1,128]{2,1,0:T(1,128)}, u32[]{:S(2)}, u32[]{:S(2)}) collective-permute-start(f32[192,1,128]{2,1,0:T(1,128)} %get-tuple-element.48), channel_id=1, source_target_pairs={{1,0},{0,1},{3,2},{2,3},{5,4},{4,5},{7,6},{6,7},{9,8},{8,9},{11,10... | collective-permute-start | bytes 294920 | tf_op jit(solution)/shard_map/ppermute | solution.py:25
  19.7 3.8 %copy-start.4 = (f32[32,128]{1,0:T(8,128)S(1)}, f32[32,128]{1,0:T(8,128)}, u32[]{:S(2)}) copy-start(f32[32,128]{1,0:T(8,128)} %param.3) | copy-start | bytes 49156
  23.5 111.1 %copy-start.5 = (f32[32,128]{1,0:T(8,128)}, f32[32,128]{1,0:T(8,128)S(1)}, u32[]{:S(2)}) copy-start(f32[32,128]{1,0:T(8,128)S(1)} %broadcast_add_fusion) | copy-start | bytes 49156
  88.0 3.4 %copy-start.3 = (f32[4,32,128]{2,0,1:T(4,128)S(1)}, f32[4,32,128]{2,0,1:T(4,128)}, u32[]{:S(2)}) copy-start(f32[4,32,128]{2,0,1:T(4,128)} %all-reduce.2.cloned.1.call-done) | copy-start | bytes 196612
  88.0 3.4 %copy-start.2 = (f32[192,32,127]{2,1,0:T(8,128)S(1)}, f32[192,32,127]{2,1,0:T(8,128)}, u32[]{:S(2)}) copy-start(f32[192,32,127]{2,1,0:T(8,128)} %get-tuple-element.43) | copy-start | bytes 9363460
  88.8 1.4 collective-permute-start
  88.8 1.4 collective-permute-start.1
  97.7 1.7 copy-start.1
  138.8 1.7 collective-permute-start.4
  138.9 1.6 collective-permute-start.5
  182.8 5.6 %collective-permute-start.6 = (f32[4,32,128]{2,0,1:T(4,128)}, f32[4,32,128]{2,0,1:T(4,128)S(1)}, u32[]{:S(2)}, u32[]{:S(2)}) collective-permute-start(f32[4,32,128]{2,0,1:T(4,128)} %get-tuple-element.25), channel_id=1, source_target_pairs={{0,16},{1,17},{2,18},{3,19},{4,20},{5,21},{6,22},{7,23},{8,24},{9,... | collective-permute-start | bytes 196616 | tf_op jit(solution)/shard_map/ppermute | solution.py:33
  188.4 1.2 collective-permute-start.7
  188.5 1.3 collective-permute-start.8
Sparse Core Ops, SparseCore 0:
  16.0 71.9 all-reduce.1
